TPU v7x, 128 devices: a whole 4x4x4 slice. The times are simulated.
128 devices in a mesh: gx: 8 (over y, core), gy: 16 (over z, x).
Axes of the slice: x: 4, y: 4, z: 4, core: 2. Of those that a mesh axis runs over, the one named last changes fastest.
Arguments:
- positions: float32 [3, 2097152], P(None, ('gx', 'gy')), may hold values from 0 to 128, as said below
- point_feat: float32 [32, 2097152], P(None, ('gx', 'gy')), may hold values from -1.8 to 1.8
- area: float32 [2097152], P(('gx', 'gy')), may hold values from 0.3 to 3
- block_brick: int32 [16384], P(('gx', 'gy')), may hold values from 0 to 4095, as said below
- block_count: int32 [128], P(('gx', 'gy')), may hold values from 8 to 128, as said below
- sdf: float32 [128, 128, 128], P('gx', 'gy'), may hold values from -6 to 6
- grid_gain: float32 [32], replicated, may hold values from -4 to 4
- mix_w: float32 [2, 32, 32], replicated, may hold values from -1 to 1
- mix_b: float32 [2, 32], replicated, may hold values from -1.8 to 1.8
- spec_w: float32 [2, 2, 16, 32, 1024], P(None, None, 'gy', 'gx'), may hold values from -18 to 18
- readout_w: float32 [32], replicated, may hold values from -1 to 1
Outputs:
- pressure: float32 [2097152], P(('gx', 'gy'))
Inputs may be any that keep to these rules, and one draw needn't show every extreme that they name: `block_brick`: block n belongs to partition d = n // 128. Its brick b lies in the grid pencil row of that partition: (b // 256) // 2 == d // 16. Of the blocks of one partition at most 8 lie in the bricks of one pencil, the pencil of b being ((b // 16) % 16); in every pencil row some pencil holds exactly 8 of the first 8 blocks of every partition of that row. The live blocks of partition d are its first block_count[d] blocks; some partition has all 128 live and some has exactly 8. `positions`: every point lies inside its block's brick, 0.5 or more from each of the brick's faces.
All inputs are finite; a program needn't handle non-finite values.
Results may differ from a plain program's by a relative error of at most 0.0003.
Values sent between devices are 32-bit elements; how exact they have to be, the bound alone decides.
A program may use at most 128 MiB of HBM per device.

v0:
```python
import jax
import jax.numpy as jnp
from jax import lax
from jax.sharding import PartitionSpec as P

G = 128
M = 32
B = 8
KZ = 16


highest = lax.Precision.HIGHEST


def phase_table(length, frequency):
    places = jnp.arange(length, dtype=jnp.int32)
    wrapped = jnp.mod(places[:, None] * frequency[None, :], length).astype(jnp.float32)
    phases = wrapped * (2.0 * jnp.pi / length)
    return (jnp.cos(phases), jnp.sin(phases))


def kept_freqs(mode_count):
    mode_index = jnp.arange(mode_count, dtype=jnp.int32)
    return jnp.where(mode_index < mode_count // 2, mode_index, mode_index - mode_count)


def cell_offsets(brick_edge):
    cell_index = jnp.arange(brick_edge * brick_edge * brick_edge, dtype=jnp.int32)
    coords = jnp.stack(
        [
            cell_index // (brick_edge * brick_edge),
            cell_index // brick_edge % brick_edge,
            cell_index % brick_edge,
        ]
    )
    return coords.astype(jnp.float32) + 0.5


def kernel_weights(corners, points, offsets, radius):
    distance = jnp.zeros((corners.shape[0], offsets.shape[1], points.shape[2]), dtype=jnp.float32)
    for axis_id in range(3):
        centre_line = corners[:, axis_id][:, None] + offsets[axis_id][None, :]
        gap_line = centre_line[:, :, None] - points[:, axis_id][:, None, :]
        distance = distance + gap_line * gap_line
    return jnp.square(jnp.maximum(1.0 - distance / (radius * radius), 0.0))


def rotate(spectra, table_cos, table_sin, pattern, direction):
    part_real = spectra[0]
    part_imag = spectra[1]
    real_cos = jnp.einsum(pattern, part_real, table_cos, precision=highest)
    real_sin = jnp.einsum(pattern, part_real, table_sin, precision=highest)
    imag_cos = jnp.einsum(pattern, part_imag, table_cos, precision=highest)
    imag_sin = jnp.einsum(pattern, part_imag, table_sin, precision=highest)
    return jnp.stack([real_cos - direction * imag_sin, imag_cos + direction * real_sin])


def spectral_part(grid_field, weights, tables):
    z_cos, z_sin, f_cos, f_sin, inv_cos, inv_sin, back_cos, back_sin = tables
    part_real = jnp.einsum("cxyz,zk->kcxy", grid_field, z_cos, precision=highest)
    part_imag = -jnp.einsum("cxyz,zk->kcxy", grid_field, z_sin, precision=highest)
    spectra = jnp.stack([part_real, part_imag])
    spectra = lax.all_to_all(spectra, "gy", split_axis=1, concat_axis=4, tiled=True)
    spectra = rotate(spectra, f_cos, f_sin, "...y,ym->...m", -1.0)
    spectra = lax.all_to_all(spectra, "gx", split_axis=2, concat_axis=3, tiled=True)
    spectra = rotate(spectra, f_cos, f_sin, "...xm,xn->...nm", -1.0)
    wave_shape = spectra.shape
    flattened = spectra.reshape(2, wave_shape[1], wave_shape[2], wave_shape[3] * wave_shape[4])
    prod_real = flattened[0] * weights[0] - flattened[1] * weights[1]
    prod_imag = flattened[0] * weights[1] + flattened[1] * weights[0]
    spectra = jnp.stack([prod_real, prod_imag]).reshape(wave_shape)
    spectra = rotate(spectra, inv_cos, inv_sin, "...nm,xn->...xm", 1.0)
    spectra = lax.all_to_all(spectra, "gx", split_axis=3, concat_axis=2, tiled=True)
    spectra = rotate(spectra, inv_cos, inv_sin, "...m,ym->...y", 1.0)
    spectra = lax.all_to_all(spectra, "gy", split_axis=4, concat_axis=1, tiled=True)
    result_real = jnp.einsum("kcxy,zk->cxyz", spectra[0], back_cos, precision=highest)
    result_imag = jnp.einsum("kcxy,zk->cxyz", spectra[1], back_sin, precision=highest)
    return result_real - result_imag


def per_device(
    positions,
    point_feat,
    area,
    block_brick,
    block_count,
    sdf,
    grid_gain,
    mix_w,
    mix_b,
    spec_w,
    readout_w,
):
    row_x = lax.axis_index("gx")
    row_y = lax.axis_index("gy")
    owners = lax.axis_size("gy")
    brick_edge = B
    side_bricks = G // brick_edge
    bricks_x = side_bricks // lax.axis_size("gx")
    bricks_y = side_bricks // owners
    block_total = block_brick.shape[0]
    capacity = block_total // owners
    block_points = positions.shape[1] // block_total
    channels = point_feat.shape[0]
    cell_count = brick_edge * brick_edge * brick_edge
    group_size = 4
    live_mask = jnp.arange(block_total, dtype=jnp.int32) < block_count[0]
    target = block_brick // side_bricks % side_bricks // bricks_y
    choose = (
        (target[:, None] == jnp.arange(owners, dtype=jnp.int32)[None, :]) & live_mask[:, None]
    ).astype(jnp.int32)
    before = jnp.cumsum(choose, axis=0) - choose
    order_in = jnp.sum(before * choose, axis=1)
    slot_of = target * capacity + order_in
    send_index = jnp.where(live_mask, slot_of, block_total)
    block_pos = positions.reshape(3, block_total, block_points).transpose(1, 0, 2)
    block_feat = point_feat.reshape(channels, block_total, block_points).transpose(1, 0, 2)
    block_area = area.reshape(block_total, 1, block_points)
    stacked = jnp.concatenate([block_pos, block_feat, block_area], axis=1)
    outgoing = jnp.zeros_like(stacked).at[send_index].set(stacked, mode="drop")
    incoming = lax.all_to_all(outgoing, "gy", split_axis=0, concat_axis=0, tiled=True)
    in_pos = incoming[:, 0:3, :]
    in_feat = incoming[:, 3 : 3 + channels, :] * incoming[:, 3 + channels : 4 + channels, :]
    home_brick = jnp.floor(in_pos[:, :, 0] / brick_edge).astype(jnp.int32)
    brick_xi = jnp.clip(home_brick[:, 0] - row_x * bricks_x, 0, bricks_x - 1)
    brick_yi = jnp.clip(home_brick[:, 1] - row_y * bricks_y, 0, bricks_y - 1)
    brick_zi = jnp.clip(home_brick[:, 2], 0, side_bricks - 1)
    local_id = (brick_xi * bricks_y + brick_yi) * side_bricks + brick_zi
    corners = (
        jnp.stack(
            [row_x * bricks_x + brick_xi, row_y * bricks_y + brick_yi, brick_zi], axis=1
        ).astype(jnp.float32)
        * brick_edge
    )
    local_count = bricks_x * bricks_y * side_bricks
    picker = (local_id[:, None] == jnp.arange(local_count, dtype=jnp.int32)[None, :]).astype(
        jnp.float32
    )
    offsets = cell_offsets(brick_edge)
    group_count = block_total // group_size
    corner_groups = corners.reshape(group_count, group_size, 3)
    point_groups = in_pos.reshape(group_count, group_size, 3, block_points)

    def encode_group(group_items):
        corner_set, point_set, feature_set = group_items
        weights = kernel_weights(corner_set, point_set, offsets, brick_edge)
        return jnp.einsum("rcp,rgp->rcg", feature_set, weights, precision=highest)

    contrib = lax.map(
        encode_group,
        (
            corner_groups,
            point_groups,
            in_feat.reshape(group_count, group_size, channels, block_points),
        ),
    )
    contrib = contrib.reshape(block_total, channels * cell_count)
    local_bricks = jnp.einsum("rb,rf->bf", picker, contrib, precision=highest)
    grid_field = local_bricks.reshape(
        bricks_x, bricks_y, side_bricks, channels, brick_edge, brick_edge, brick_edge
    )
    grid_field = grid_field.transpose(3, 0, 4, 1, 5, 2, 6).reshape(
        channels, bricks_x * brick_edge, bricks_y * brick_edge, G
    )
    grid_field = grid_field + grid_gain[:, None, None, None] * sdf[None]
    z_cos, z_sin = phase_table(G, jnp.arange(KZ, dtype=jnp.int32))
    f_cos, f_sin = phase_table(G, kept_freqs(M))
    z_back = jnp.where(jnp.arange(KZ) == 0, 1.0, 2.0).astype(jnp.float32) / G
    tables = (
        z_cos,
        z_sin,
        f_cos,
        f_sin,
        f_cos / G,
        f_sin / G,
        z_cos * z_back[None, :],
        z_sin * z_back[None, :],
    )
    layers = mix_w.shape[0]
    for layer_index in range(layers):
        spectral = spectral_part(grid_field, spec_w[layer_index], tables)
        mixed_sum = jnp.einsum("oc,cxyz->oxyz", mix_w[layer_index], grid_field, precision=highest)
        mixed_sum = mixed_sum + mix_b[layer_index][:, None, None, None] + spectral
        grid_field = jax.nn.gelu(mixed_sum) if layer_index < layers - 1 else mixed_sum
    final_bricks = grid_field.reshape(
        channels, bricks_x, brick_edge, bricks_y, brick_edge, side_bricks, brick_edge
    )
    final_bricks = final_bricks.transpose(1, 3, 5, 0, 2, 4, 6).reshape(
        local_count, channels * cell_count
    )
    slot_values = final_bricks[local_id]
    slot_values = slot_values.reshape(group_count, group_size, channels, cell_count)

    def decode_group(group_items):
        corner_set, point_set, value_set = group_items
        weights = kernel_weights(corner_set, point_set, offsets, brick_edge)
        weight_sum = jnp.sum(weights, axis=1)
        safe_sum = jnp.where(weight_sum > 0.0, weight_sum, 1.0)
        return (
            jnp.einsum("rcg,rgp->rcp", value_set, weights, precision=highest) / safe_sum[:, None, :]
        )

    decoded = lax.map(decode_group, (corner_groups, point_groups, slot_values)).reshape(
        block_total, channels, block_points
    )
    reduced = jnp.einsum("c,rcp->rp", readout_w, decoded, precision=highest)
    returned = lax.all_to_all(reduced, "gy", split_axis=0, concat_axis=0, tiled=True)
    per_block = returned[slot_of]
    pressure = jnp.where(live_mask[:, None], per_block, 0.0)
    return pressure.reshape(block_total * block_points)


def solution(mesh):
    placed = (
        P(None, ("gx", "gy")),
        P(None, ("gx", "gy")),
        P(("gx", "gy")),
        P(("gx", "gy")),
        P(("gx", "gy")),
        P("gx", "gy", None),
        P(),
        P(),
        P(),
        P(None, None, "gy", "gx", None),
        P(),
    )
    return jax.shard_map(
        per_device, mesh=mesh, in_specs=placed, out_specs=P(("gx", "gy")), check_vma=False
    )
```

profile of v0, /device:TPU:0, one launch (start us, length us, event | category | flops | bytes accessed | tf_op | source)
XLA Modules:
  0.0 728.5 jit_solution(11661430643005815858)
XLA Ops:
  6.8 16.8 %scatter_fusion = f32[128,36,128]{2,1,0:T(8,128)} fusion(f32[128,36,128]{2,1,0:T(8,128)} %broadcast_in_dim.75, s32[128]{0:T(128)S(1)} %get-tuple-element.246, f32[128,36,128]{2,1,0:T(8,128)} %pad_maximum_fusion), kind=kCustom, calls=%fused_computation.2 | custom fusion | bytes 7078400 | tf_op jit(solution)/shard_map/scatter | solution.py:120
  23.6 8.0 %all-to-all-start = ((f32[128,36,128]{2,1,0:T(8,128)}), f32[128,36,128]{2,1,0:T(8,128)}, u32[]{:S(2)}, u32[]{:S(2)}) async-start(f32[128,36,128]{2,1,0:T(8,128)} %scatter_fusion), calls=%async_computation | async-start | bytes 5242880 | tf_op jit(solution)/shard_map/all_to_all | solution.py:121
  32.6 41.2 %all-to-all-done = f32[128,36,128]{2,1,0:T(8,128)} async-done(((f32[128,36,128]{2,1,0:T(8,128)}), f32[128,36,128]{2,1,0:T(8,128)}, u32[]{:S(2)}, u32[]{:S(2)}) %all-to-all-start) | async-done | bytes 2359328 | tf_op jit(solution)/shard_map/all_to_all | solution.py:121
  81.5 124.8 %while.20 = (s32[]{:T(128)}, f32[32,4,32,512]{3,2,1,0:T(8,128)}, f32[32,4,32,128]{3,2,1,0:T(8,128)}, f32[32,4,3]{2,1,0:T(4,128)S(1)}, f32[3,512]{1,0:T(4,128)S(1)}, /*index=5*/f32[32,4,3,128]{3,1,2,0:T(4,128)S(1)}, s32[]{:T(128)}) while((s32[]{:T(128)}, f32[32,4,32,512]{3,2,1,0:T(8,128)}, f32[32,4,32,128]{3,2,1,0:T(8,128)}, ...), condition=%wide.region_4.5_spmd, body=%wide.region_3.4_spmd.sunk | while | flops 103815168 | bytes 427333 | solution.py:149
  81.8 3.5 fusion.504
  89.6 3.5 fusion.504
  93.5 3.5 fusion.504
  97.4 3.5 fusion.504
  101.3 3.5 fusion.504
  105.2 3.5 fusion.504
  109.1 3.5 fusion.504
  113.0 3.6 fusion.504
  116.9 3.5 fusion.504
  120.8 3.6 fusion.504
  124.7 3.5 fusion.504
  132.5 3.6 fusion.504
  136.4 3.6 fusion.504
  140.3 3.5 fusion.504
  148.1 3.5 fusion.504
  152.0 3.6 fusion.504
  155.9 3.5 fusion.504
  159.8 3.5 fusion.504
  163.7 3.5 fusion.504
  167.6 3.5 fusion.504
  175.4 3.6 fusion.504
  179.3 3.6 fusion.504
  183.2 3.6 fusion.504
  187.1 3.5 fusion.504
  191.0 3.6 fusion.504
  194.9 3.6 fusion.504
  198.9 3.5 fusion.504
  206.3 13.4 %copy.636 = f32[16,8,32,512]{3,1,2,0:T(8,128)} copy(f32[16,8,32,512]{3,2,1,0:T(8,128)} %bitcast.489) | data formatting | bytes 16777216
  219.7 9.0 %copy.528 = f32[16384,128]{1,0:T(8,128)} copy(f32[16384,128]{0,1:T(8,128)} %bitcast.479) | data formatting | bytes 16777216 | tf_op jit(solution)/shard_map/rb,rf->bf/dot_general | solution.py:158
  228.7 23.7 %multiply_add_fusion = (f32[32,2,8,1,8,16,8]{0,5,6,4,2,1,3:T(8,128)}, f32[32,2,8,1,8,16,8]{0,5,6,4,2,1,3:T(8,128)S(1)}) fusion(f32[2,8,8,16,8]{3,4,2,1,0:T(8,128)S(1)} %copy.530, f32[32]{0:T(128)S(1)} %copy-done.9, f32[32,8,8,8,128]{4,3,2,1,0:T(8,128)} %bitcast.478, s32[2,16]{1,0:T(2,128)S(1)} %multiply_add_fusion.2, s32[128]{0:T(128)S(1)} %bitcast.548), kind=kOutput, calls=%fused_computation.78 | convolution fusion | flops 806359040 | bytes 12649216 | tf_op jit(solution)/shard_map/rb,rf->bf/dot_general | solution.py:158
  252.4 7.3 %copy.533 = f32[32,2,8,1,8,16,8]{0,6,5,4,2,1,3:T(8,128)} copy(f32[32,2,8,1,8,16,8]{0,5,6,4,2,1,3:T(8,128)S(1)} %get-tuple-element.250) | data formatting | bytes 4194304 | tf_op jit(solution)/shard_map/transpose | solution.py:162
  259.8 6.9 copy.534
  268.5 8.4 %fusion.75 = f32[1,16,32,16,8]{2,1,4,3,0:T(8,128)S(1)} fusion(f32[32,16,8,128]{3,2,1,0:T(8,128)S(1)} %multiply_add_fusion.1), kind=kOutput, calls=%fused_computation.112 | convolution fusion | flops 100691968 | bytes 2359296 | tf_op jit(solution)/shard_map/cxyz,zk->kcxy/dot_general | solution.py:60
  276.9 8.4 %fusion.81 = f32[1,16,32,16,8]{2,1,4,3,0:T(8,128)S(1)} fusion(f32[32,16,8,128]{3,2,1,0:T(8,128)S(1)} %multiply_add_fusion.1), kind=kOutput, calls=%fused_computation.114 | convolution fusion | flops 100757504 | bytes 2359296 | tf_op jit(solution)/shard_map/cxyz,zk->kcxy/dot_general | solution.py:61
  287.9 4.1 all-to-all-start.1
  292.1 11.2 %all-to-all-done.1 = f32[16,1,8192]{2,1,0:T(1,128)S(1)} async-done(((f32[16,1,8192]{2,1,0:T(1,128)}), f32[16,1,8192]{2,1,0:T(1,128)S(1)}, u32[]{:S(2)}, u32[]{:S(2)}) %all-to-all-start.1) | async-done | bytes 524320 | tf_op jit(solution)/shard_map/all_to_all | solution.py:63
  318.8 5.8 all-to-all-done.2
  333.6 6.0 all-to-all-done.3
  346.8 4.0 all-to-all-start.4
  350.8 7.5 %copy.531 = f32[32,2,8,1,8,16,8]{0,6,5,4,2,1,3:T(8,128)S(1)} copy(f32[32,2,8,1,8,16,8]{0,5,6,4,2,1,3:T(8,128)} %get-tuple-element.249) | data formatting | bytes 4194304 | tf_op jit(solution)/shard_map/add | solution.py:165
  358.3 10.1 %fusion.118 = f32[16,8,128,32]{2,3,1,0:T(8,128)} fusion(f32[32,16,8,128]{0,3,2,1:T(8,128)S(1)} %bitcast.477, f32[2,32,32]{2,1,0:T(8,128)S(1)} %copy-done.8), kind=kOutput, calls=%fused_computation.192 | convolution fusion | flops 201326592 | bytes 10502144 | tf_op jit(solution)/shard_map/oc,cxyz->oxyz/dot_general | solution.py:182
  371.2 4.5 copy.560
  381.5 3.8 fusion.58
  385.3 8.2 %convolution_bitcast_fusion.1 = f32[1,16,32,16,8]{2,1,4,3,0:T(8,128)S(1)} fusion(f32[32,16,8,128]{3,0,2,1:T(8,128)S(1)} %fusion.58), kind=kOutput, calls=%fused_computation.117 | convolution fusion | flops 100691968 | bytes 2359296 | tf_op jit(solution)/shard_map/cxyz,zk->kcxy/dot_general | solution.py:60
  393.5 8.6 %fusion.84 = f32[1,16,32,16,8]{2,1,4,3,0:T(8,128)S(1)} fusion(f32[32,16,8,128]{3,0,2,1:T(8,128)S(1)} %fusion.58), kind=kOutput, calls=%fused_computation.116 | convolution fusion | flops 100757504 | bytes 2359296 | tf_op jit(solution)/shard_map/cxyz,zk->kcxy/dot_general | solution.py:61
  406.8 18.0 %all_to_all.134 = f32[16,1,8192]{2,1,0:T(1,128)S(1)} all-to-all(f32[16,1,8192]{2,1,0:T(1,128)S(1)} %reshape.783), channel_id=1, replica_groups=mesh['gx'=8,'gy'=16] {'gy'}, dimensions={0} | all-to-all | bytes 1048576 | tf_op jit(solution)/shard_map/all_to_all | solution.py:63
  442.8 5.9 all-to-all-done.6
  453.6 8.7 %all_to_all.135 = f32[8,1,4096]{2,1,0:T(1,128)S(1)} all-to-all(f32[8,1,4096]{2,1,0:T(1,128)S(1)} %reshape.787), channel_id=1, replica_groups=mesh['gx'=8,'gy'=16] {'gx'}, dimensions={0} | all-to-all | bytes 262144 | tf_op jit(solution)/shard_map/all_to_all | solution.py:73
  471.7 3.6 all-to-all-start.8
  478.5 8.3 %all-to-all-done.8 = f32[16,1,8192]{2,1,0:T(1,128)S(1)} async-done(((f32[16,1,8192]{2,1,0:T(1,128)}), f32[16,1,8192]{2,1,0:T(1,128)S(1)}, u32[]{:S(2)}, u32[]{:S(2)}) %all-to-all-start.8) | async-done | bytes 524320 | tf_op jit(solution)/shard_map/all_to_all | solution.py:75
  489.4 4.7 copy.586
  503.2 4.7 copy.589
  507.8 26.7 %copy.590 = f32[2,1,16,32,8,8,8]{2,0,6,5,4,3,1:T(2,128)} copy(f32[2,1,16,32,8,8,8]{3,6,2,5,4,0,1:T(8,128)} %bitcast.475) | data formatting | bytes 4194304 | tf_op jit(solution)/shard_map/transpose | solution.py:188
  534.5 16.3 %reshape.693 = f32[32,16384]{0,1:T(8,128)} reshape(f32[2,1,16,32,8,8,8]{2,0,6,5,4,3,1:T(2,128)} %copy.590) | data formatting | bytes 4194304 | tf_op jit(solution)/shard_map/reshape | solution.py:188
  550.9 5.4 copy.591
  556.3 6.1 gather_fusion
  562.3 13.1 %copy.637 = f32[16,8,32,512]{3,2,1,0:T(8,128)} copy(f32[16,8,32,512]{3,1,2,0:T(8,128)} %bitcast.480) | data formatting | bytes 16777216
  575.4 136.6 %while.21 = (s32[]{:T(128)}, f32[32,4,32,128]{3,2,1,0:T(8,128)}, f32[32,4,32,512]{3,2,1,0:T(8,128)}, f32[32,4,3]{2,1,0:T(4,128)S(1)}, f32[3,512]{1,0:T(4,128)S(1)}, /*index=5*/f32[32,4,3,128]{3,1,2,0:T(4,128)S(1)}, s32[]{:T(128)}) while((s32[]{:T(128)}, f32[32,4,32,128]{3,2,1,0:T(8,128)}, f32[32,4,32,512]{3,2,1,0:T(8,128)}, ...), condition=%wide.region_7.8_spmd, body=%wide.region_5.7_spmd.sunk | while | flops 107239936 | bytes 466245 | solution.py:203
  712.1 3.6 fusion.271
  719.2 7.6 %all-to-all-done.9 = f32[16,8,128]{2,1,0:T(8,128)S(1)} async-done(((f32[16,8,128]{2,1,0:T(8,128)}), f32[16,8,128]{2,1,0:T(8,128)S(1)}, u32[]{:S(2)}, u32[]{:S(2)}) %all-to-all-start.9) | async-done | bytes 65568 | tf_op jit(solution)/shard_map/all_to_all | solution.py:207
  (738 shorter events, 280.2 us)
Async XLA Ops:
  0.0 1.9 copy-start
  0.8 1.4 copy-start.10
  1.9 0.7 copy-start.15
  1.9 1.2 copy-start.5
  1.9 1.2 copy-start.6
  23.6 8.1 %copy-start.4 = (f32[16,8,128]{2,1,0:T(8,128)S(1)}, f32[16,8,128]{2,1,0:T(8,128)}, u32[]{:S(2)}) copy-start(f32[16,8,128]{2,1,0:T(8,128)} %param.20) | copy-start | bytes 196612
  23.6 50.2 %all-to-all-start = ((f32[128,36,128]{2,1,0:T(8,128)}), f32[128,36,128]{2,1,0:T(8,128)}, u32[]{:S(2)}, u32[]{:S(2)}) async-start(f32[128,36,128]{2,1,0:T(8,128)} %scatter_fusion), calls=%async_computation | async-start | bytes 5242880 | tf_op jit(solution)/shard_map/all_to_all | solution.py:121
  219.7 9.0 %copy-start.9 = (f32[32]{0:T(128)S(1)}, f32[32]{0:T(128)}, u32[]{:S(2)}) copy-start(f32[32]{0:T(128)} %param.21) | copy-start | bytes 388
  287.9 15.4 %all-to-all-start.1 = ((f32[16,1,8192]{2,1,0:T(1,128)}), f32[16,1,8192]{2,1,0:T(1,128)S(1)}, u32[]{:S(2)}, u32[]{:S(2)}) async-start(f32[16,1,8192]{2,1,0:T(1,128)} %reshape.775), calls=%async_computation.1 | async-start | bytes 1048576 | tf_op jit(solution)/shard_map/all_to_all | solution.py:63
  312.1 6.5 copy-start.7
  315.2 9.4 %all-to-all-start.2 = ((f32[8,1,4096]{2,1,0:T(1,128)}), f32[8,1,4096]{2,1,0:T(1,128)S(1)}, u32[]{:S(2)}, u32[]{:S(2)}) async-start(f32[8,1,4096]{2,1,0:T(1,128)} %reshape.777), calls=%async_computation.2 | async-start | bytes 262144 | tf_op jit(solution)/shard_map/all_to_all | solution.py:65
  326.6 7.0 copy-start.13
  330.2 9.4 %all-to-all-start.3 = ((f32[8,1,4096]{2,1,0:T(1,128)}), f32[8,1,4096]{2,1,0:T(1,128)S(1)}, u32[]{:S(2)}, u32[]{:S(2)}) async-start(f32[8,1,4096]{2,1,0:T(1,128)} %reshape.779), calls=%async_computation.3 | async-start | bytes 262144 | tf_op jit(solution)/shard_map/all_to_all | solution.py:73
  346.8 21.7 %all-to-all-start.4 = ((f32[16,1,8192]{2,1,0:T(1,128)}), f32[16,1,8192]{2,1,0:T(1,128)S(1)}, u32[]{:S(2)}, u32[]{:S(2)}) async-start(f32[16,1,8192]{2,1,0:T(1,128)} %reshape.781), calls=%async_computation.4 | async-start | bytes 1048576 | tf_op jit(solution)/shard_map/all_to_all | solution.py:75
  350.8 7.5 %copy-start.8 = (f32[2,32,32]{2,1,0:T(8,128)S(1)}, f32[2,32,32]{2,1,0:T(8,128)}, u32[]{:S(2)}) copy-start(f32[2,32,32]{2,1,0:T(8,128)} %param.22) | copy-start | bytes 24580
  378.3 3.2 copy-start.2
  439.2 9.4 %all-to-all-start.6 = ((f32[8,1,4096]{2,1,0:T(1,128)}), f32[8,1,4096]{2,1,0:T(1,128)S(1)}, u32[]{:S(2)}, u32[]{:S(2)}) async-start(f32[8,1,4096]{2,1,0:T(1,128)} %reshape.785), calls=%async_computation.6 | async-start | bytes 262144 | tf_op jit(solution)/shard_map/all_to_all | solution.py:65
  471.7 15.2 %all-to-all-start.8 = ((f32[16,1,8192]{2,1,0:T(1,128)}), f32[16,1,8192]{2,1,0:T(1,128)S(1)}, u32[]{:S(2)}, u32[]{:S(2)}) async-start(f32[16,1,8192]{2,1,0:T(1,128)} %reshape.789), calls=%async_computation.8 | async-start | bytes 1048576 | tf_op jit(solution)/shard_map/all_to_all | solution.py:75
  496.7 3.2 copy-start.3
  575.4 136.7 %copy-start.14 = (f32[32]{0:T(128)S(1)}, f32[32]{0:T(128)}, u32[]{:S(2)}) copy-start(f32[32]{0:T(128)} %param.25) | copy-start | bytes 388
  712.0 7.1 copy-start.12
  712.0 15.3 %copy-start.11 = (pred[128]{0:T(512)(128)(4,1)S(1)}, pred[128]{0:T(512)(128)(4,1)}, u32[]{:S(2)}) copy-start(pred[128]{0:T(512)(128)(4,1)} %copy-done.10) | copy-start | bytes 388
  712.0 16.1 %copy-start.1 = (f32[32,16384]{1,0:T(8,128)S(1)}, f32[32,16384]{1,0:T(8,128)}, u32[]{:S(2)}) copy-start(f32[32,16384]{1,0:T(8,128)} %param.16) | copy-start | bytes 6291460
  715.6 11.1 %all-to-all-start.9 = ((f32[16,8,128]{2,1,0:T(8,128)}), f32[16,8,128]{2,1,0:T(8,128)S(1)}, u32[]{:S(2)}, u32[]{:S(2)}) async-start(f32[16,8,128]{2,1,0:T(8,128)} %bitcast.175), calls=%async_computation.9 | async-start | bytes 131072 | tf_op jit(solution)/shard_map/all_to_all | solution.py:207
where the time goes:
time: 742 us; the launch traced here: 729 us
  matrix products  319 us (43%)
  local copies, waits for them, and re-layouts  197 us (27%)
  waiting for transfers between devices  86 us (12%)
  other arithmetic  63.6 us (9%)
  starting transfers between devices  33.3 us (4%)
  blocking collectives  26.7 us (4%)
    dot_general x32, matrix products, encode_group(): return jnp.einsum('rcp,rgp->rcg', feature_set, weights, precision=highest)  113 us
    dot_general x32, matrix products, decode_group(): jnp.einsum('rcg,rgp->rcp', value_set, weights, precision=highest)  93.5 us
    unnamed x53, local copies, waits for them, and re-layouts  44.2 us
    all_to_all x1, waiting for transfers between devices, per_device(): lax.all_to_all(outgoing, 'gy', split_axis=0, concat_axis=0, tiled=True)  41.2 us
    reduce_sum x32, other arithmetic, decode_group(): weight_sum = jnp.sum(weights, axis=1)  31.4 us
    transpose x1, local copies, waits for them, and re-layouts, per_device(): final_bricks.transpose(1, 3, 5, 0, 2, 4, 6)  26.7 us
    dot_general x1, matrix products, per_device(): local_bricks = jnp.einsum('rb,rf->bf', picker, contrib, precision=highest)  23.7 us
    reshape x2, local copies, waits for them, and re-layouts, per_device(): final_bricks.transpose(1, 3, 5, 0, 2, 4, 6)  21.7 us
  transfers between devices with their start and end apart: 8, of which 7 were waited for; matrix products, arithmetic and copies ran while one was open for 3% of the time, Pallas kernels for 0%

commit v1 on v0

v1 whole, which is shorter than its diff:
```python
import functools

import jax
import jax.numpy as jnp
import ml_dtypes
import numpy as np
from jax import lax
from jax.experimental import pallas as pl
from jax.experimental.pallas import tpu as pltpu
from jax.sharding import PartitionSpec as P

MESH = pl.DeviceIdType.MESH
F32 = jnp.float32
BF16 = jnp.bfloat16

G = 128
M = 32
KZ = 16
NX = 8
NY = 16
CAP = 8
SLOTS = NY * CAP
ROWS = CAP * 32 + 3 * CAP
POINTS = [(t % 4, (t % 4 + t // 4) % 4) for t in range(16)]
FAR = [(2, 2), (2, 1), (1, 2), (2, 3), (3, 2), (1, 1), (3, 3), (3, 1), (1, 3), (2, 0), (0, 2), (0, 1), (1, 0), (0, 3), (3, 0), (0, 0)]


def split_table(table):
    high = table.astype(ml_dtypes.bfloat16)
    low = (table - high.astype(np.float64)).astype(ml_dtypes.bfloat16)
    return high, low


def tables():
    place = np.arange(G)
    kz = np.arange(KZ)
    m = np.arange(M)
    freq = np.where(m < M // 2, m, m - M)
    za = 2.0 * np.pi * (np.outer(kz, place) % G) / G
    fa = 2.0 * np.pi * (np.outer(place, freq) % G) / G
    c, s = np.cos(fa), np.sin(fa)
    zf_h, zf_l = split_table(np.concatenate([np.cos(za), -np.sin(za)], 0))
    zero = np.zeros_like(zf_h)
    zf = np.block([[zf_h, zf_h], [zf_l, zero]])
    yf_h, yf_l = split_table(np.block([[c, -s], [s, c]]))
    yf = np.block([[yf_h, yf_l], [yf_h, np.zeros_like(yf_l)]])
    xf_h, xf_l = split_table(np.concatenate([c.T, s.T], 1))
    xf = np.concatenate([xf_h, xf_l], 0)
    xi_h, xi_l = split_table(np.concatenate([c, s], 1) / G)
    xi = np.concatenate([xi_h, xi_l], 1)
    yi_h, yi_l = split_table(np.block([[c.T, s.T], [-s.T, c.T]]) / G)
    yi = np.concatenate([yi_h, yi_h, yi_l, yi_l], 0)
    back = np.where(kz == 0, 1.0, 2.0)[:, None] / G
    zi_h, zi_l = split_table(np.concatenate([np.cos(za) * back, -np.sin(za) * back], 0).T)
    zi = np.concatenate([zi_h, zi_h, zi_l, zi_l], 1)

    def spread(t):
        return np.repeat(t.reshape(G, 2, KZ).transpose(0, 2, 1), NX, axis=1).reshape(G, 2 * KZ * NX)

    zs = np.concatenate([spread(zi_h), spread(zi_h), spread(zi_l)], 1)
    return [jnp.asarray(t, BF16) for t in (zf, yf, xf, xi, yi, zi, zs)]


def dot(a, b):
    return jnp.dot(a, b, preferred_element_type=F32)


def split(value):
    high = value.astype(BF16)
    low = (value - high.astype(F32)).astype(BF16)
    return high, low


def split3(value):
    high = value.astype(BF16)
    rest = value - high.astype(F32)
    mid = rest.astype(BF16)
    return high, mid, (rest - mid.astype(F32)).astype(BF16)


def pick(chosen, value):
    return dot(chosen, jnp.concatenate(split3(value), axis=0))


def lanes(shape):
    return lax.broadcasted_iota(jnp.int32, shape, len(shape) - 1)


def split_lanes(value):
    high = value.astype(BF16).astype(F32)
    return jnp.where(lanes(value.shape) < 64, high, value - high).astype(BF16)


def fold(value):
    return value + pltpu.roll(value, 64, 1)


def swap16(tiles):
    group = lanes(tiles[0].shape) // 8
    for d in (1, 2, 4, 8):
        mask = (group // d) % 2 == 0
        new = list(tiles)
        for i in range(16):
            if i & d:
                continue
            a, b = tiles[i], tiles[i + d]
            new[i] = jnp.where(mask, a, pltpu.roll(b, 8 * d, 1))
            new[i + d] = jnp.where(mask, pltpu.roll(a, G - 8 * d, 1), b)
        tiles = new
    return tiles


def kernel_tiles(px, py, pz):
    def local(p):
        q = p * 0.125
        return jnp.broadcast_to(q - jnp.floor(q), (8, 128))

    ux, uy, uz = local(px), local(py), local(pz)
    centre = (lax.broadcasted_iota(jnp.int32, (8, 128), 0).astype(F32) + 0.5) * 0.125
    gap = centre - uy
    base = 1.0 - gap * gap
    ex, ez = [], []
    for a in range(8):
        gx = (a + 0.5) * 0.125 - ux
        ex.append(gx * gx)
        gz = (a + 0.5) * 0.125 - uz
        ez.append(base - gz * gz)
    out = []
    for z in range(8):
        for x in range(8):
            t = jnp.maximum(ez[z] - ex[x], 0.0)
            out.append(t * t)
    return out


def points_offset(t):
    step = lax.rem(t, 4)
    return step, lax.rem(step + t // 4, 4)


def mega(
    brick, count, feat, pos, area, sdf, gain, mix, bias, spec, readout, zf_h, yf_h, xf_h, xi_h, yi_h, zi_h, zs_h,
    out,
    zf, yf, xf, xi, yi, zi, zs,
    brickv, counts, posv, areav, sdfv, gains, mixv, biases, specv, readouts,
    vecv, vecs, mixf, mixt, wbuf, homes, placed,
    sbuf, rbuf, msend, mrecv, kst, contr, g, mixed, sdft,
    send, frecv, irecv, frecv1, jsend, jrecv, plane, sacc, srow, psend, precv,
    insem, featsem, bsem, psem, msem, osem, fsem, isem, f1sem, jsem, rsem, entered,
):
    gx = lax.axis_index("gx")
    gy = lax.axis_index("gy")
    me = gx * NY + gy
    cy, core = gx // 2, lax.rem(gx, 2)
    cz, cx = gy // 4, lax.rem(gy, 4)

    def peer(dz, dx):
        return lax.rem(cz + dz, 4) * 4 + lax.rem(cx + dx, 4)

    small = [
        (brick, brickv), (count, counts), (pos, posv), (area, areav), (readout, readouts), (mix, mixv), (bias, biases),
        (gain, gains), (spec, specv), (sdf, sdfv),
        (zf_h, zf), (yf_h, yf), (xf_h, xf), (xi_h, xi), (yi_h, yi), (zi_h, zi), (zs_h, zs),
    ]
    loads = [pltpu.make_async_copy(a, b, insem.at[i]) for i, (a, b) in enumerate(small)]
    for load in loads[:4]:
        load.start()

    barrier = pltpu.get_barrier_semaphore()
    for t in range(1, NY):
        pl.semaphore_signal(barrier, inc=1, device_id=(gx, lax.rem(gy + t, NY)), device_id_type=MESH)
    for t in range(1, NX):
        pl.semaphore_signal(barrier, inc=1, device_id=(lax.rem(gx + t, NX), gy), device_id_type=MESH)

    def load_feat(n, carry):
        pltpu.make_async_copy(
            feat.at[:, pl.ds(pl.multiple_of(n * 128, 128), 128)],
            mixed.at[pl.ds(pl.multiple_of(n * 32, 32), 32), :], featsem,
        ).start()
        return carry

    lax.fori_loop(0, SLOTS, load_feat, 0)
    for load in loads[4:]:
        load.start()

    sub = lax.broadcasted_iota(jnp.int32, (G, G), 0)
    lane = lanes((G, G))
    one = jnp.ones((G, G), jnp.int32)
    zero = jnp.zeros((G, G), jnp.int32)

    def total(value):
        return jnp.sum(value, axis=0, keepdims=True)

    loads[0].wait()
    loads[1].wait()
    blocks = jnp.broadcast_to(brickv[...], (G, G))
    live_blocks = counts[0]
    owner = lax.shift_right_logical(blocks, 4) & 15
    inner = (lax.shift_right_logical(blocks, 8) & 1) * 16 + (blocks & 15)
    owner_t = jnp.transpose(owner)
    ahead = (owner_t == owner) & (sub < lane) & (sub < live_blocks)
    slot = jnp.where(lane[0:1] < live_blocks, owner[0:1] * CAP + total(jnp.where(ahead, one, zero)), SLOTS)
    match = jnp.where(jnp.transpose(jnp.broadcast_to(slot, (G, G))) == lane, one, zero)
    bricks = jnp.where(total(match) > 0, total(match * jnp.transpose(inner)), 32)
    msend[...] = jnp.transpose(jnp.broadcast_to(bricks, (G, G)))
    mine = pl.ds(pl.multiple_of(gy * CAP, CAP), CAP)
    mrecv[mine, :] = msend[mine, :]
    back_home = match.astype(F32).astype(BF16)
    homes[...] = jnp.concatenate([back_home] * 3, axis=1)
    to_slot = jnp.transpose(match).astype(F32).astype(BF16)
    placed[...] = jnp.concatenate([to_slot] * 3, axis=1)

    loads[2].wait()
    loads[3].wait()
    pltpu.make_async_copy(mixed, mixed, featsem).wait()

    areas = jnp.concatenate([areav[:, 128 * n : 128 * n + 128] for n in range(SLOTS)], axis=0)
    scale = pick(placed[...], areas)

    def pack(c, carry):
        h, l = split(mixed[pl.ds(c, SLOTS, stride=32), :])
        o = dot(placed[:, 0:256], jnp.concatenate([h, l], axis=0)) * scale
        for j in range(NY):
            sbuf[j, pl.ds(c, CAP, stride=32), :] = o[CAP * j : CAP * j + CAP]
        return carry

    lax.fori_loop(0, 32, pack, 0, unroll=2)
    for k in range(3):
        o = pick(placed[...], jnp.concatenate([posv[k : k + 1, 128 * n : 128 * n + 128] for n in range(SLOTS)], axis=0))
        for j in range(NY):
            sbuf[j, 256 + 8 * k : 264 + 8 * k, :] = o[CAP * j : CAP * j + CAP]
    pl.semaphore_wait(barrier, NY + NX - 2)

    for dz, dx in POINTS[1:]:
        j = peer(dz, dx)
        pltpu.make_async_remote_copy(
            src_ref=msend.at[pl.ds(pl.multiple_of(j * CAP, CAP), CAP), :], dst_ref=mrecv.at[mine, :],
            send_sem=msem.at[0], recv_sem=msem.at[1], device_id=(gx, j), device_id_type=MESH,
        ).start()
    for dz, dx in POINTS[1:]:
        j = peer(dz, dx)
        pltpu.make_async_remote_copy(
            src_ref=sbuf.at[j], dst_ref=rbuf.at[gy],
            send_sem=bsem, recv_sem=psem.at[gy], device_id=(gx, j), device_id_type=MESH,
        ).start()
    for t in range(1, NX):
        pl.semaphore_signal(entered, inc=1, device_id=(lax.rem(gx + t, NX), gy), device_id_type=MESH)
    rbuf[gy] = sbuf[gy]

    for load in loads[4:]:
        load.wait()
    sdft[...] = jnp.transpose(sdfv[...])
    vec = jnp.zeros((1, 32), F32)
    shift = jnp.float32(0.0)
    for o in range(32):
        vec = vec + readouts[o] * mixv[1, o : o + 1, :]
        shift = shift + readouts[o] * biases[1, o]
    vecv[:, 0:32] = vec
    vec_copy = pltpu.make_async_copy(vecv, vecs, osem)
    vec_copy.start()
    for k in range(4):
        mixf[:, 32 * k : 32 * k + 32] = mixv[0]
    mixt[...] = split_lanes(mixf[...])
    narrow = lanes((8, 128)) < 32
    for layer in range(2):
        pair = jnp.concatenate([specv[2 * layer], specv[2 * layer + 1]], axis=0)
        for t in range(8):
            part = pair[:, 128 * t : 128 * t + 128]
            for u in range(4):
                w = jnp.where(narrow, part if u == 0 else pltpu.roll(part, G - 32 * u, 1), 0.0)
                w = w + pltpu.roll(w, 32, 1)
                wbuf[layer * 256 + (4 * t + u) * 8 : layer * 256 + (4 * t + u) * 8 + 8, :] = w + pltpu.roll(w, 64, 1)
    vec_copy.wait()

    whole = mrecv.at[pl.ds(0, (NY - 1) * CAP), :]
    pltpu.make_async_copy(whole, whole, msem.at[0]).wait()
    pltpu.make_async_copy(whole, whole, msem.at[1]).wait()
    inside = jnp.where(jnp.transpose(mrecv[...])[0:32] == sub[0:32], 1.0, 0.0).astype(BF16)
    inside = jnp.concatenate([inside, inside], axis=1)

    def encode(t, carry):
        dz, dx = points_offset(t)
        j = lax.rem(cz + 4 - dz, 4) * 4 + lax.rem(cx + 4 - dx, 4)

        @pl.when(t > 0)
        def _():
            pltpu.make_async_copy(rbuf.at[j], rbuf.at[j], psem.at[j]).wait()

        for i in range(CAP):
            tiles = kernel_tiles(
                rbuf[j, 256 + i : 257 + i, :], rbuf[j, 264 + i : 265 + i, :], rbuf[j, 272 + i : 273 + i, :]
            )
            kh, kl = split(jnp.concatenate(tiles, axis=0))
            fh, fl = split(rbuf[j, 32 * i : 32 * i + 32, :])
            lhs = jnp.concatenate(
                [jnp.concatenate([fh, fh], axis=1), jnp.concatenate([fl, jnp.zeros_like(fl)], axis=1)], axis=0
            )
            rhs = jnp.concatenate([kh, kl], axis=1)
            kst[j * CAP + i] = rhs
            o = lax.dot_general(lhs, rhs, (((1,), (1,)), ((), ())), preferred_element_type=F32)
            o = o[0:32] + o[32:64]
            for q in range(4):
                contr[q, pl.ds(pl.multiple_of((j * CAP + i) * 32, 32), 32), :] = o[:, 128 * q : 128 * q + 128]
        return carry

    lax.fori_loop(0, NY, encode, 0)

    low = lanes((16, 128)) < 64

    def assemble(c, carry):
        for q in range(4):
            h, l = split(contr[q, pl.ds(c, SLOTS, stride=32), :])
            o = dot(inside, jnp.concatenate([h, l], axis=0))
            a, b = o[0:16], o[16:32]
            g[pl.ds(c * G + 2 * q, 16, stride=8), :] = jnp.where(low, a, pltpu.roll(b, 64, 1))
            g[pl.ds(c * G + 2 * q + 1, 16, stride=8), :] = jnp.where(low, pltpu.roll(a, 64, 1), b)
        return carry

    lax.fori_loop(0, 32, assemble, 0, unroll=2)
    pl.semaphore_wait(entered, NX - 1)

    def group_of(t):
        u = t // 2
        dy = lax.rem(2 + 3 * u + 3 * (u // 2) + 2 * (u // 3), 4)
        return lax.rem(cy + dy, 4) * 2 + lax.rem(core + 1 + lax.rem(t, 2), 2)

    partners = [peer(dz, dx) for dz, dx in FAR]

    def issue(t, grp, source_row, recv, row, size, sem):
        for n, k in enumerate(partners):
            copy = pltpu.make_async_remote_copy(
                src_ref=send.at[pl.ds(pl.multiple_of(source_row(k), size), size), :] if size == 8
                else jsend.at[pl.ds(pl.multiple_of(source_row(k), size), size), :],
                dst_ref=recv.at[pl.ds(pl.multiple_of(row, size), size), :],
                send_sem=sem.at[0], recv_sem=sem.at[1], device_id=(grp, k), device_id_type=MESH,
            )
            if n < NY - 1:
                copy.start()
            else:
                pl.when(t < NX - 1)(copy.start)

    def forward(recv, sem, prepare):
        def group(t, carry):
            grp = group_of(t)
            for ci in range(4):
                c = grp * 4 + ci
                rows = pl.ds(pl.multiple_of(c * G, G), G)
                value = prepare(c, rows)
                h, l = split(value)
                o = dot(zf[...], jnp.concatenate([h, l], axis=0))
                o = o[0:32] + o[32:64]
                for ri in range(2):
                    send[pl.ds(grp * 8 + ri * 4 + ci, 16, stride=64), :] = o[16 * ri : 16 * ri + 16]
            issue(t, grp, lambda k: (k * NX + grp) * 8, recv, me * 8, 8, sem)
            return carry

        lax.fori_loop(0, NX, group, 0)
        recv[pl.ds(pl.multiple_of(me * 8, 8), 8), :] = send[pl.ds(pl.multiple_of((gy * NX + gx) * 8, 8), 8), :]

    def arrive(recv, sem, size=8):
        part = recv.at[pl.ds(0, (NX * NY - 1) * size), :]
        pltpu.make_async_copy(part, part, sem.at[1]).wait()
        pltpu.make_async_copy(part, part, sem.at[0]).wait()

    sign_f = jnp.where(lanes((1, 128)) % 64 < 32, 1.0, -1.0)

    def modes(recv, layer):
        for a in range(NX):
            tiles = [recv[(a * 16 + b) * 8 : (a * 16 + b) * 8 + 8, :] for b in range(16)]
            tiles = swap16(tiles)
            for b in range(16):
                plane[(a * 16 + b) * 8 : (a * 16 + b) * 8 + 8, :] = tiles[b]
        result = []
        for ci in range(4):
            both = jnp.concatenate(
                [plane[pl.ds(ci, G, stride=8), :], plane[pl.ds(4 + ci, G, stride=8), :]], axis=1
            )
            h, l = split(both)
            y = fold(dot(jnp.concatenate([h, l], axis=1), yf[...]))
            y2 = pltpu.roll(y, 96, 1) * sign_f
            z = dot(xf[...], jnp.concatenate([split_lanes(y), split_lanes(y2)], axis=0))
            z = fold(z[0:32] + z[32:64])
            wr = wbuf[pl.ds(layer * 256 + ci, M, stride=8), :]
            wi = wbuf[pl.ds(layer * 256 + 4 + ci, M, stride=8), :]
            result.append(z * wr - pltpu.roll(z, 96, 1) * (wi * sign_f))
        return result

    def inverse_plane(p):
        p2 = pltpu.roll(p, 96, 1) * (-sign_f)
        r = jnp.concatenate([split_lanes(p), split_lanes(p2)], axis=0)
        q = split_lanes(fold(dot(xi[...], jnp.concatenate([r, r], axis=0))))
        return dot(jnp.concatenate([q, q], axis=1), yi[...])

    def prepare0(c, rows):
        value = g[rows, :] + gains[c] * sdft[...]
        g[rows, :] = value
        return value

    forward(frecv, fsem, prepare0)

    def mix_cells(z, carry):
        h, l = split(g[pl.ds(z, 32, stride=G), :])
        mixed[pl.ds(z, 32, stride=G), :] = dot(mixt[...], jnp.concatenate([h, l, h, l], axis=0))
        return carry

    lax.fori_loop(0, G, mix_cells, 0, unroll=4)
    arrive(frecv, fsem)
    for ci, p in enumerate(modes(frecv, 0)):
        o = inverse_plane(p)
        plane[pl.ds(ci, G, stride=8), :] = o[:, 0:128]
        plane[pl.ds(ci + 4, G, stride=8), :] = o[:, 128:256]

    spot = gy * NX + gx

    def back(t, carry):
        grp = group_of(t)
        base = pl.multiple_of(grp * 128, 128)
        tiles = swap16([plane[pl.ds(base + 8 * b, 8), :] for b in range(16)])
        for b in range(16):
            send[pl.ds(base + 8 * b, 8), :] = tiles[b]
        issue(t, grp, lambda k: (grp * NY + k) * 8, irecv, spot * 8, 8, isem)
        return carry

    lax.fori_loop(0, NX, back, 0)
    irecv[pl.ds(pl.multiple_of(spot * 8, 8), 8), :] = send[pl.ds(pl.multiple_of(me * 8, 8), 8), :]
    arrive(irecv, isem)
    sacc[...] = jnp.zeros_like(sacc) + shift

    def prepare1(c, rows):
        grp, ci = c // 4, lax.rem(c, 4)
        re = irecv[pl.ds(grp * 8 + ci, 16, stride=64), :]
        im = irecv[pl.ds(grp * 8 + 4 + ci, 16, stride=64), :]
        h, l = split(jnp.concatenate([re, im], axis=0))
        value = dot(zi[...], jnp.concatenate([h, l, h, l], axis=0)) + mixed[rows, :] + biases[0, c]
        value = jax.nn.gelu(value)
        sacc[...] += vecs[0, c] * value
        return value

    forward(frecv1, f1sem, prepare1)
    arrive(frecv1, f1sem)
    projected = None
    for ci, p in enumerate(modes(frecv1, 1)):
        p = p * readouts[gx * 4 + ci]
        projected = p if projected is None else projected + p
    o = inverse_plane(projected)
    for a in range(NX):
        for ri in range(2):
            plane[pl.ds((a // 4) * 128 + (a % 4) * 2 + ri, 16, stride=8), :] = o[16 * a : 16 * a + 16, 128 * ri : 128 * ri + 128]
    for half in range(2):
        tiles = swap16([plane[half * 128 + 8 * b : half * 128 + 8 * b + 8, :] for b in range(16)])
        for b in range(16):
            jsend[half * 128 + 8 * b : half * 128 + 8 * b + 8, :] = tiles[b]

    def back1(t, carry):
        grp = group_of(t)
        issue(t, grp, lambda k: ((grp // 4) * 16 + k) * 8 + lax.rem(grp, 4) * 2, jrecv, spot * 2, 2, jsem)
        return carry

    lax.fori_loop(0, NX, back1, 0)
    jrecv[pl.ds(pl.multiple_of(spot * 2, 2), 2), :] = jsend[
        pl.ds(pl.multiple_of(((gx // 4) * 16 + gy) * 8 + lax.rem(gx, 4) * 2, 2), 2), :
    ]
    arrive(jrecv, jsem, 2)
    h, l = split(jrecv[...])
    field = sacc[...] + dot(zs[...], jnp.concatenate([h, l, h], axis=0))

    left = lanes((16, 128)) < 64
    sacc[...] = field
    for q in range(4):
        a = sacc[pl.ds(2 * q, 16, stride=8), :]
        b = sacc[pl.ds(2 * q + 1, 16, stride=8), :]
        for bx in range(2):
            w = jnp.where(left, a, pltpu.roll(b, 64, 1)) if bx == 0 else jnp.where(left, pltpu.roll(a, 64, 1), b)
            h, l = split(w)
            srow[16 * bx : 16 * bx + 16, 128 * q : 128 * q + 128] = h
            srow[32 + 16 * bx : 48 + 16 * bx, 128 * q : 128 * q + 128] = l
    srow[64:80, :] = jnp.ones((16, 512), BF16)
    which = sub[0:32]

    def decode(j, carry):
        nums, dens = [], []
        for i in range(CAP):
            o = dot(srow[...], kst[j * CAP + i])
            o = o[0:72, 0:128] + o[0:72, 128:256]
            owned = jnp.broadcast_to(mrecv[pl.ds(j * CAP + i, 1), :], (32, 128)) == which
            nums.append(total(jnp.where(owned, o[0:32] + o[32:64], 0.0)))
            dens.append(o[64:65])
        psend[pl.ds(pl.multiple_of(j * CAP, CAP), CAP), :] = jnp.concatenate(nums, axis=0) / jnp.concatenate(dens, axis=0)
        return carry

    lax.fori_loop(0, NY, decode, 0)
    precv[mine, :] = psend[mine, :]
    for dz, dx in FAR[:-1]:
        j = peer(dz, dx)
        pltpu.make_async_remote_copy(
            src_ref=psend.at[pl.ds(pl.multiple_of(j * CAP, CAP), CAP), :], dst_ref=precv.at[mine, :],
            send_sem=rsem.at[0], recv_sem=rsem.at[1], device_id=(gx, j), device_id_type=MESH,
        ).start()
    part = precv.at[pl.ds(0, (NY - 1) * CAP), :]
    pltpu.make_async_copy(part, part, rsem.at[1]).wait()
    pltpu.make_async_copy(part, part, rsem.at[0]).wait()
    sent = sbuf.at[pl.ds(0, NY - 1)]
    pltpu.make_async_copy(sent, sent, bsem).wait()

    out[...] = pick(homes[...], precv[...])


def per_device(positions, point_feat, area, block_brick, block_count, sdf, grid_gain, mix_w, mix_b, spec_w, readout_w):
    consts = tables()
    hbm = pl.BlockSpec(memory_space=pl.ANY)
    dma = pltpu.SemaphoreType.DMA
    vmem = pltpu.VMEM
    i32 = jnp.int32
    out = pl.pallas_call(
        mega,
        out_shape=jax.ShapeDtypeStruct((SLOTS, 128), F32),
        in_specs=[hbm] * (11 + len(consts)),
        out_specs=pl.BlockSpec(memory_space=vmem),
        scratch_shapes=[vmem(t.shape, BF16) for t in consts]
        + [
            vmem((1, SLOTS), i32),
            pltpu.SMEM((1,), i32),
            vmem((3, SLOTS * 128), F32),
            vmem((1, SLOTS * 128), F32),
            vmem((G, 128), F32),
            pltpu.SMEM((32,), F32),
            vmem((2, 32, 32), F32),
            pltpu.SMEM((2, 32), F32),
            vmem((4, 4, M * M), F32),
            pltpu.SMEM((32,), F32),
            vmem((1, 128), F32),
            pltpu.SMEM((1, 128), F32),
            vmem((32, 128), F32),
            vmem((32, 128), BF16),
            vmem((512, 128), F32),
            vmem((SLOTS, 384), BF16),
            vmem((SLOTS, 384), BF16),
            vmem((NY, ROWS, 128), F32),
            vmem((NY, ROWS, 128), F32),
            vmem((SLOTS, 128), i32),
            vmem((SLOTS, 128), i32),
            vmem((SLOTS, 512, 256), BF16),
            vmem((4, SLOTS * 32, 128), F32),
            vmem((32 * G, 128), F32),
            vmem((32 * G, 128), F32),
            vmem((G, 128), F32),
            vmem((1024, 128), F32),
            vmem((1024, 128), F32),
            vmem((1024, 128), F32),
            vmem((1024, 128), F32),
            vmem((256, 128), F32),
            vmem((256, 128), F32),
            vmem((1024, 128), F32),
            vmem((G, 128), F32),
            vmem((80, 512), BF16),
            vmem((SLOTS, 128), F32),
            vmem((SLOTS, 128), F32),
            dma((10 + len(consts),)), dma, dma, dma((NY,)), dma((2,)), dma, dma((2,)), dma((2,)), dma((2,)),
            dma((2,)), dma((2,)), pltpu.SemaphoreType.REGULAR,
        ],
        compiler_params=pltpu.CompilerParams(collective_id=0, has_side_effects=True, vmem_limit_bytes=67043328),
        name="operator",
    )(
        block_brick.reshape(1, SLOTS), block_count, point_feat, positions, area.reshape(1, SLOTS * 128), sdf.reshape(G, 128),
        grid_gain, mix_w, mix_b, spec_w.reshape(4, 4, M * M), readout_w, *consts,
    )
    return out.reshape(SLOTS * 128)


def solution(mesh):
    placed = (
        P(None, ("gx", "gy")),
        P(None, ("gx", "gy")),
        P(("gx", "gy")),
        P(("gx", "gy")),
        P(("gx", "gy")),
        P("gx", "gy", None),
        P(),
        P(),
        P(),
        P(None, None, "gy", "gx", None),
        P(),
    )
    return jax.shard_map(per_device, mesh=mesh, in_specs=placed, out_specs=P(("gx", "gy")), check_vma=False)
```

time: 742 us -> 112 us (0.15); the launches traced: 729 us -> 111 us
  matrix products: 319 us -> 0 us
  local copies, waits for them, and re-layouts: 197 us -> 1.47 us
  Pallas kernels: 0 us -> 109 us
  waiting for transfers between devices: 86 us -> 0 us
  other arithmetic: 63.6 us -> 0 us
  starting transfers between devices: 33.3 us -> 0 us
  blocking collectives: 26.7 us -> 0 us
    dot_general x100 -> x0, matrix products: 316 us -> none  [the longest x32 113 us: encode_group(): return jnp.einsum('rcp,rgp->rcg', feature_set, weights, precision=highest)]
    pallas_call x0 -> x1, Pallas kernels: none -> 109 us  [per_device(): pl.pallas_call(mega, out_shape=jax.ShapeDtypeStruct((SLOTS, 128), F32), i...]
    all_to_all x8 -> x0, waiting for transfers between devices: 86 us -> none  [the longest x1 41.2 us: per_device(): lax.all_to_all(outgoing, 'gy', split_axis=0, concat_axis=0, tiled=True)]
    unnamed x53 -> x1, local copies, waits for them, and re-layouts: 44.2 us -> 1.47 us
    transpose x3 -> x0, local copies, waits for them, and re-layouts: 34.3 us -> none  [the longest x1 26.7 us: per_device(): final_bricks.transpose(1, 3, 5, 0, 2, 4, 6)]
    all_to_all x8 -> x0, starting transfers between devices: 33.3 us -> none  [the longest x1 8.02 us: per_device(): lax.all_to_all(outgoing, 'gy', split_axis=0, concat_axis=0, tiled=True)]
    reduce_sum x33 -> x0, other arithmetic: 31.4 us -> none  [the longest x32 31.4 us: decode_group(): weight_sum = jnp.sum(weights, axis=1)]
    reshape x3 -> x0, local copies, waits for them, and re-layouts: 28.6 us -> none  [the longest x2 21.7 us: per_device(): final_bricks.transpose(1, 3, 5, 0, 2, 4, 6)]
  transfers between devices with their start and end apart: 8 -> 0, of which waited for: 7 -> 0; matrix products, arithmetic and copies ran while one was open for 3% -> 0% of each run, Pallas kernels for 0% -> 0%
where the time goes in v1:
time: 112 us; the launch traced here: 111 us
  Pallas kernels  109 us (97%)
  local copies, waits for them, and re-layouts  1.47 us (1%)
    pallas_call x1, Pallas kernels, per_device(): pl.pallas_call(mega, out_shape=jax.ShapeDtypeStruct((SLOTS, 128), F32), i...  109 us

profile of v1, /device:TPU:0, one launch (start us, length us, event | category | flops | bytes accessed | tf_op | source)
XLA Modules:
  0.0 111.4 jit_solution(1235980848227043968)
XLA Ops:
  0.7 109.3 %operator.1 = f32[128,128]{1,0:T(8,128)} custom-call(s32[1,128]{1,0:T(1,128)} %bitcast.9, s32[1]{0:T(128)S(6)} %copy.20.count, f32[32,16384]{1,0:T(8,128)} %feat.1, f32[3,16384]{1,0:T(4,128)} %pos.1, f32[1,16384]{1,0:T(1,128)} %bitcast.6, f32[128,128]{1,0:T(8,128)} %bitcast.7, f32[32]{0:T(128)} %gain.1, f32[2,32,32]{2,1,0:T(8,128)} %mix.1, f32[2,32]{1,0:T(2,128)} %bias.1, ...), custom_call_target="tpu_custom_call" | custom-call | tf_op jit(solution)/shard_map/operator/pallas_call | solution.py:514
  109.9 1.5 %copy.21 = f32[16384]{0:T(1024)} copy(f32[16384]{0:T(1024)} %bitcast.5) | data formatting | bytes 131072

commit v2 on v1

--- a/solution.py
+++ b/solution.py
@@ -39,9 +39,11 @@
     za = 2.0 * np.pi * (np.outer(kz, place) % G) / G
     fa = 2.0 * np.pi * (np.outer(place, freq) % G) / G
     c, s = np.cos(fa), np.sin(fa)
-    zf_h, zf_l = split_table(np.concatenate([np.cos(za), -np.sin(za)], 0))
-    zero = np.zeros_like(zf_h)
-    zf = np.block([[zf_h, zf_h], [zf_l, zero]])
+    kept = (place % 16) * 8 + place // 16
+    four = np.eye(4)
+    zt = np.stack([np.cos(za), -np.sin(za)], 1)[:, :, kept]
+    zf_h, zf_l = split_table(np.einsum("krz,cd->krcdz", zt, four).reshape(8 * KZ, 4 * G))
+    zf = np.concatenate([zf_h, zf_h, zf_l], 1)
     yf_h, yf_l = split_table(np.block([[c, -s], [s, c]]))
     yf = np.block([[yf_h, yf_l], [yf_h, np.zeros_like(yf_l)]])
     xf_h, xf_l = split_table(np.concatenate([c.T, s.T], 1))
@@ -51,13 +53,11 @@
     yi_h, yi_l = split_table(np.block([[c.T, s.T], [-s.T, c.T]]) / G)
     yi = np.concatenate([yi_h, yi_h, yi_l, yi_l], 0)
     back = np.where(kz == 0, 1.0, 2.0)[:, None] / G
-    zi_h, zi_l = split_table(np.concatenate([np.cos(za) * back, -np.sin(za) * back], 0).T)
-    zi = np.concatenate([zi_h, zi_h, zi_l, zi_l], 1)
-
-    def spread(t):
-        return np.repeat(t.reshape(G, 2, KZ).transpose(0, 2, 1), NX, axis=1).reshape(G, 2 * KZ * NX)
-
-    zs = np.concatenate([spread(zi_h), spread(zi_h), spread(zi_l)], 1)
+    zb = zt * back[:, :, None]
+    zi_h, zi_l = split_table(np.einsum("krz,cd->czkrd", zb, four).reshape(4 * G, 8 * KZ))
+    zi = np.concatenate([zi_h, zi_h, zi_l], 1)
+    zs_h, zs_l = split_table(np.repeat(zb.transpose(2, 0, 1), NX, axis=1).reshape(G, 2 * KZ * NX))
+    zs = np.concatenate([zs_h, zs_h, zs_l], 1)
     return [jnp.asarray(t, BF16) for t in (zf, yf, xf, xi, yi, zi, zs)]
 
 
@@ -69,6 +69,21 @@
     high = value.astype(BF16)
     low = (value - high.astype(F32)).astype(BF16)
     return high, low
+
+
+def swap8(tiles):
+    row = lax.broadcasted_iota(jnp.int32, (8, 128), 0)
+    for d in (1, 2, 4):
+        mask = (row // d) % 2 == 0
+        new = list(tiles)
+        for i in range(8):
+            if i & d:
+                continue
+            a, b = tiles[i], tiles[i + d]
+            new[i] = jnp.where(mask, a, pltpu.roll(b, d, 0))
+            new[i + d] = jnp.where(mask, pltpu.roll(a, 8 - d, 0), b)
+        tiles = new
+    return tiles
 
 
 def split3(value):
@@ -175,7 +190,7 @@
     def load_feat(n, carry):
         pltpu.make_async_copy(
             feat.at[:, pl.ds(pl.multiple_of(n * 128, 128), 128)],
-            mixed.at[pl.ds(pl.multiple_of(n * 32, 32), 32), :], featsem,
+            mixed.at[:, n, :], featsem,
         ).start()
         return carry
 
@@ -218,10 +233,10 @@
     scale = pick(placed[...], areas)
 
     def pack(c, carry):
-        h, l = split(mixed[pl.ds(c, SLOTS, stride=32), :])
+        h, l = split(mixed[c])
         o = dot(placed[:, 0:256], jnp.concatenate([h, l], axis=0)) * scale
         for j in range(NY):
-            sbuf[j, pl.ds(c, CAP, stride=32), :] = o[CAP * j : CAP * j + CAP]
+            sbuf[j, pl.ds(pl.multiple_of(c * CAP, CAP), CAP), :] = o[CAP * j : CAP * j + CAP]
         return carry
 
     lax.fori_loop(0, 32, pack, 0, unroll=2)
@@ -249,7 +264,9 @@
 
     for load in loads[4:]:
         load.wait()
-    sdft[...] = jnp.transpose(sdfv[...])
+    sacc[...] = jnp.transpose(sdfv[...])
+    for a in range(8):
+        sdft[16 * a : 16 * a + 16, :] = sacc[pl.ds(a, 16, stride=8), :]
     vec = jnp.zeros((1, 32), F32)
     shift = jnp.float32(0.0)
     for o in range(32):
@@ -286,21 +303,26 @@
         def _():
             pltpu.make_async_copy(rbuf.at[j], rbuf.at[j], psem.at[j]).wait()
 
+        outs = []
         for i in range(CAP):
             tiles = kernel_tiles(
                 rbuf[j, 256 + i : 257 + i, :], rbuf[j, 264 + i : 265 + i, :], rbuf[j, 272 + i : 273 + i, :]
             )
             kh, kl = split(jnp.concatenate(tiles, axis=0))
-            fh, fl = split(rbuf[j, 32 * i : 32 * i + 32, :])
+            fh, fl = split(rbuf[j, pl.ds(i, 32, stride=CAP), :])
             lhs = jnp.concatenate(
                 [jnp.concatenate([fh, fh], axis=1), jnp.concatenate([fl, jnp.zeros_like(fl)], axis=1)], axis=0
             )
             rhs = jnp.concatenate([kh, kl], axis=1)
             kst[j * CAP + i] = rhs
             o = lax.dot_general(lhs, rhs, (((1,), (1,)), ((), ())), preferred_element_type=F32)
-            o = o[0:32] + o[32:64]
+            outs.append(o[0:32] + o[32:64])
+        for b in range(4):
             for q in range(4):
-                contr[q, pl.ds(pl.multiple_of((j * CAP + i) * 32, 32), 32), :] = o[:, 128 * q : 128 * q + 128]
+                turned = swap8([outs[i][8 * b : 8 * b + 8, 128 * q : 128 * q + 128] for i in range(CAP)])
+                for i in range(CAP):
+                    row = pl.multiple_of((8 * b + i) * SLOTS + j * CAP, CAP)
+                    contr[q, pl.ds(row, CAP), :] = turned[i]
         return carry
 
     lax.fori_loop(0, NY, encode, 0)
@@ -309,11 +331,12 @@
 
     def assemble(c, carry):
         for q in range(4):
-            h, l = split(contr[q, pl.ds(c, SLOTS, stride=32), :])
+            h, l = split(contr[q, pl.ds(pl.multiple_of(c * SLOTS, SLOTS), SLOTS), :])
             o = dot(inside, jnp.concatenate([h, l], axis=0))
             a, b = o[0:16], o[16:32]
-            g[pl.ds(c * G + 2 * q, 16, stride=8), :] = jnp.where(low, a, pltpu.roll(b, 64, 1))
-            g[pl.ds(c * G + 2 * q + 1, 16, stride=8), :] = jnp.where(low, pltpu.roll(a, 64, 1), b)
+            row = pl.multiple_of(c * G + 32 * q, 32)
+            g[pl.ds(row, 16), :] = jnp.where(low, a, pltpu.roll(b, 64, 1))
+            g[pl.ds(row + 16, 16), :] = jnp.where(low, pltpu.roll(a, 64, 1), b)
         return carry
 
     lax.fori_loop(0, 32, assemble, 0, unroll=2)
@@ -342,20 +365,14 @@
     def forward(recv, sem, prepare):
         def group(t, carry):
             grp = group_of(t)
-            for ci in range(4):
-                c = grp * 4 + ci
-                rows = pl.ds(pl.multiple_of(c * G, G), G)
-                value = prepare(c, rows)
-                h, l = split(value)
-                o = dot(zf[...], jnp.concatenate([h, l], axis=0))
-                o = o[0:32] + o[32:64]
-                for ri in range(2):
-                    send[pl.ds(grp * 8 + ri * 4 + ci, 16, stride=64), :] = o[16 * ri : 16 * ri + 16]
-            issue(t, grp, lambda k: (k * NX + grp) * 8, recv, me * 8, 8, sem)
+            h, l = split(jnp.concatenate(prepare(grp), axis=0))
+            rows = pl.ds(pl.multiple_of(grp * 128, 128), 128)
+            send[rows, :] = dot(zf[...], jnp.concatenate([h, l, h], axis=0))
+            issue(t, grp, lambda k: (grp * NY + k) * 8, recv, me * 8, 8, sem)
             return carry
 
         lax.fori_loop(0, NX, group, 0)
-        recv[pl.ds(pl.multiple_of(me * 8, 8), 8), :] = send[pl.ds(pl.multiple_of((gy * NX + gx) * 8, 8), 8), :]
+        recv[pl.ds(pl.multiple_of(me * 8, 8), 8), :] = send[pl.ds(pl.multiple_of(me * 8, 8), 8), :]
 
     def arrive(recv, sem, size=8):
         part = recv.at[pl.ds(0, (NX * NY - 1) * size), :]
@@ -370,45 +387,63 @@
             tiles = swap16(tiles)
             for b in range(16):
                 plane[(a * 16 + b) * 8 : (a * 16 + b) * 8 + 8, :] = tiles[b]
+        both = jnp.concatenate(
+            [
+                jnp.concatenate([plane[pl.ds(ci, G, stride=8), :], plane[pl.ds(4 + ci, G, stride=8), :]], axis=1)
+                for ci in range(4)
+            ],
+            axis=0,
+        )
+        h, l = split(both)
+        y = fold(dot(jnp.concatenate([h, l], axis=1), yf[...]))
+        y2 = pltpu.roll(y, 96, 1) * sign_f
+        r = [
+            jnp.concatenate([split_lanes(y[G * ci : G * ci + G]), split_lanes(y2[G * ci : G * ci + G])], axis=0)
+            for ci in range(4)
+        ]
+        z4 = dot(xf[...], jnp.concatenate(r, axis=1))
+        z4 = z4[0:32] + z4[32:64]
         result = []
         for ci in range(4):
-            both = jnp.concatenate(
-                [plane[pl.ds(ci, G, stride=8), :], plane[pl.ds(4 + ci, G, stride=8), :]], axis=1
-            )
-            h, l = split(both)
-            y = fold(dot(jnp.concatenate([h, l], axis=1), yf[...]))
-            y2 = pltpu.roll(y, 96, 1) * sign_f
-            z = dot(xf[...], jnp.concatenate([split_lanes(y), split_lanes(y2)], axis=0))
-            z = fold(z[0:32] + z[32:64])
+            z = fold(z4[:, 128 * ci : 128 * ci + 128])
             wr = wbuf[pl.ds(layer * 256 + ci, M, stride=8), :]
             wi = wbuf[pl.ds(layer * 256 + 4 + ci, M, stride=8), :]
             result.append(z * wr - pltpu.roll(z, 96, 1) * (wi * sign_f))
         return result
 
-    def inverse_plane(p):
-        p2 = pltpu.roll(p, 96, 1) * (-sign_f)
-        r = jnp.concatenate([split_lanes(p), split_lanes(p2)], axis=0)
-        q = split_lanes(fold(dot(xi[...], jnp.concatenate([r, r], axis=0))))
+    def inverse_planes(parts):
+        r = []
+        for p in parts:
+            pair = jnp.concatenate([split_lanes(p), split_lanes(pltpu.roll(p, 96, 1) * (-sign_f))], axis=0)
+            r.append(jnp.concatenate([pair, pair], axis=0))
+        q4 = dot(xi[...], jnp.concatenate(r, axis=1))
+        q = jnp.concatenate([split_lanes(fold(q4[:, 128 * n : 128 * n + 128])) for n in range(len(parts))], axis=0)
         return dot(jnp.concatenate([q, q], axis=1), yi[...])
 
-    def prepare0(c, rows):
-        value = g[rows, :] + gains[c] * sdft[...]
-        g[rows, :] = value
-        return value
+    def prepare0(grp):
+        values = []
+        for ci in range(4):
+            rows = pl.ds(pl.multiple_of((grp * 4 + ci) * G, G), G)
+            value = g[rows, :] + gains[grp * 4 + ci] * sdft[...]
+            g[rows, :] = value
+            values.append(value)
+        return values
 
     forward(frecv, fsem, prepare0)
+
+    mixed2 = mixed.reshape(32 * G, 128)
 
     def mix_cells(z, carry):
         h, l = split(g[pl.ds(z, 32, stride=G), :])
-        mixed[pl.ds(z, 32, stride=G), :] = dot(mixt[...], jnp.concatenate([h, l, h, l], axis=0))
+        mixed2[pl.ds(z, 32, stride=G), :] = dot(mixt[...], jnp.concatenate([h, l, h, l], axis=0))
         return carry
 
     lax.fori_loop(0, G, mix_cells, 0, unroll=4)
     arrive(frecv, fsem)
-    for ci, p in enumerate(modes(frecv, 0)):
-        o = inverse_plane(p)
-        plane[pl.ds(ci, G, stride=8), :] = o[:, 0:128]
-        plane[pl.ds(ci + 4, G, stride=8), :] = o[:, 128:256]
+    o = inverse_planes(modes(frecv, 0))
+    for ci in range(4):
+        plane[pl.ds(ci, G, stride=8), :] = o[G * ci : G * ci + G, 0:128]
+        plane[pl.ds(ci + 4, G, stride=8), :] = o[G * ci : G * ci + G, 128:256]
 
     spot = gy * NX + gx
 
@@ -418,23 +453,26 @@
         tiles = swap16([plane[pl.ds(base + 8 * b, 8), :] for b in range(16)])
         for b in range(16):
             send[pl.ds(base + 8 * b, 8), :] = tiles[b]
-        issue(t, grp, lambda k: (grp * NY + k) * 8, irecv, spot * 8, 8, isem)
+        issue(t, grp, lambda k: (grp * NY + k) * 8, irecv, me * 8, 8, isem)
         return carry
 
     lax.fori_loop(0, NX, back, 0)
-    irecv[pl.ds(pl.multiple_of(spot * 8, 8), 8), :] = send[pl.ds(pl.multiple_of(me * 8, 8), 8), :]
+    irecv[pl.ds(pl.multiple_of(me * 8, 8), 8), :] = send[pl.ds(pl.multiple_of(me * 8, 8), 8), :]
     arrive(irecv, isem)
     sacc[...] = jnp.zeros_like(sacc) + shift
 
-    def prepare1(c, rows):
-        grp, ci = c // 4, lax.rem(c, 4)
-        re = irecv[pl.ds(grp * 8 + ci, 16, stride=64), :]
-        im = irecv[pl.ds(grp * 8 + 4 + ci, 16, stride=64), :]
-        h, l = split(jnp.concatenate([re, im], axis=0))
-        value = dot(zi[...], jnp.concatenate([h, l, h, l], axis=0)) + mixed[rows, :] + biases[0, c]
-        value = jax.nn.gelu(value)
-        sacc[...] += vecs[0, c] * value
-        return value
+    def prepare1(grp):
+        h, l = split(irecv[pl.ds(pl.multiple_of(grp * 128, 128), 128), :])
+        spectral = dot(zi[...], jnp.concatenate([h, l, h], axis=0))
+        values = []
+        added = None
+        for ci in range(4):
+            c = grp * 4 + ci
+            value = jax.nn.gelu(spectral[G * ci : G * ci + G] + mixed[c] + biases[0, c])
+            added = vecs[0, c] * value if added is None else added + vecs[0, c] * value
+            values.append(value)
+        sacc[...] += added
+        return values
 
     forward(frecv1, f1sem, prepare1)
     arrive(frecv1, f1sem)
@@ -442,7 +480,7 @@
     for ci, p in enumerate(modes(frecv1, 1)):
         p = p * readouts[gx * 4 + ci]
         projected = p if projected is None else projected + p
-    o = inverse_plane(projected)
+    o = inverse_planes([projected])
     for a in range(NX):
         for ri in range(2):
             plane[pl.ds((a // 4) * 128 + (a % 4) * 2 + ri, 16, stride=8), :] = o[16 * a : 16 * a + 16, 128 * ri : 128 * ri + 128]
@@ -465,10 +503,9 @@
     field = sacc[...] + dot(zs[...], jnp.concatenate([h, l, h], axis=0))
 
     left = lanes((16, 128)) < 64
-    sacc[...] = field
     for q in range(4):
-        a = sacc[pl.ds(2 * q, 16, stride=8), :]
-        b = sacc[pl.ds(2 * q + 1, 16, stride=8), :]
+        a = field[32 * q : 32 * q + 16]
+        b = field[32 * q + 16 : 32 * q + 32]
         for bx in range(2):
             w = jnp.where(left, a, pltpu.roll(b, 64, 1)) if bx == 0 else jnp.where(left, pltpu.roll(a, 64, 1), b)
             h, l = split(w)
@@ -542,7 +579,7 @@
             vmem((SLOTS, 512, 256), BF16),
             vmem((4, SLOTS * 32, 128), F32),
             vmem((32 * G, 128), F32),
-            vmem((32 * G, 128), F32),
+            vmem((32, G, 128), F32),
             vmem((G, 128), F32),
             vmem((1024, 128), F32),
             vmem((1024, 128), F32),

time: 112 us -> 105 us (0.938)
  Pallas kernels: 109 us -> 103 us
    pallas_call x1, Pallas kernels: 109 us -> 103 us  [per_device(): pl.pallas_call(mega, out_shape=jax.ShapeDtypeStruct((SLOTS, 128), F32), i...]
where the time goes in v2:
time: 105 us
  Pallas kernels  103 us (98%)
  local copies, waits for them, and re-layouts  1.47 us (1%)
    pallas_call x1, Pallas kernels, per_device(): pl.pallas_call(mega, out_shape=jax.ShapeDtypeStruct((SLOTS, 128), F32), i...  103 us

profile of v2, /device:TPU:0, one launch (start us, length us, event | category | flops | bytes accessed | tf_op | source)
XLA Modules:
  0.0 104.6 jit_solution(12176889457863773914)
XLA Ops:
  0.7 102.5 %operator.1 = f32[128,128]{1,0:T(8,128)} custom-call(s32[1,128]{1,0:T(1,128)} %bitcast.9, s32[1]{0:T(128)S(6)} %copy.20.count, f32[32,16384]{1,0:T(8,128)} %feat.1, f32[3,16384]{1,0:T(4,128)} %pos.1, f32[1,16384]{1,0:T(1,128)} %bitcast.6, f32[128,128]{1,0:T(8,128)} %bitcast.7, f32[32]{0:T(128)} %gain.1, f32[2,32,32]{2,1,0:T(8,128)} %mix.1, f32[2,32]{1,0:T(2,128)} %bias.1, ...), custom_call_target="tpu_custom_call" | custom-call | tf_op jit(solution)/shard_map/operator/pallas_call | solution.py:551
  103.2 1.5 %copy.21 = f32[16384]{0:T(1024)} copy(f32[16384]{0:T(1024)} %bitcast.5) | data formatting | bytes 131072

commit v3 on v2

--- a/solution.py
+++ b/solution.py
@@ -328,18 +328,6 @@
     lax.fori_loop(0, NY, encode, 0)
 
     low = lanes((16, 128)) < 64
-
-    def assemble(c, carry):
-        for q in range(4):
-            h, l = split(contr[q, pl.ds(pl.multiple_of(c * SLOTS, SLOTS), SLOTS), :])
-            o = dot(inside, jnp.concatenate([h, l], axis=0))
-            a, b = o[0:16], o[16:32]
-            row = pl.multiple_of(c * G + 32 * q, 32)
-            g[pl.ds(row, 16), :] = jnp.where(low, a, pltpu.roll(b, 64, 1))
-            g[pl.ds(row + 16, 16), :] = jnp.where(low, pltpu.roll(a, 64, 1), b)
-        return carry
-
-    lax.fori_loop(0, 32, assemble, 0, unroll=2)
     pl.semaphore_wait(entered, NX - 1)
 
     def group_of(t):
@@ -423,9 +411,16 @@
     def prepare0(grp):
         values = []
         for ci in range(4):
-            rows = pl.ds(pl.multiple_of((grp * 4 + ci) * G, G), G)
-            value = g[rows, :] + gains[grp * 4 + ci] * sdft[...]
-            g[rows, :] = value
+            c = grp * 4 + ci
+            pieces = []
+            for q in range(4):
+                h, l = split(contr[q, pl.ds(pl.multiple_of(c * SLOTS, SLOTS), SLOTS), :])
+                o = dot(inside, jnp.concatenate([h, l], axis=0))
+                a, b = o[0:16], o[16:32]
+                pieces.append(jnp.where(low, a, pltpu.roll(b, 64, 1)))
+                pieces.append(jnp.where(low, pltpu.roll(a, 64, 1), b))
+            value = jnp.concatenate(pieces, axis=0) + gains[c] * sdft[...]
+            g[pl.ds(pl.multiple_of(c * G, G), G), :] = value
             values.append(value)
         return values
 
@@ -438,7 +433,7 @@
         mixed2[pl.ds(z, 32, stride=G), :] = dot(mixt[...], jnp.concatenate([h, l, h, l], axis=0))
         return carry
 
-    lax.fori_loop(0, G, mix_cells, 0, unroll=4)
+    lax.fori_loop(0, G // 2, mix_cells, 0, unroll=4)
     arrive(frecv, fsem)
     o = inverse_planes(modes(frecv, 0))
     for ci in range(4):
@@ -458,6 +453,7 @@
 
     lax.fori_loop(0, NX, back, 0)
     irecv[pl.ds(pl.multiple_of(me * 8, 8), 8), :] = send[pl.ds(pl.multiple_of(me * 8, 8), 8), :]
+    lax.fori_loop(G // 2, G, mix_cells, 0, unroll=4)
     arrive(irecv, isem)
     sacc[...] = jnp.zeros_like(sacc) + shift
 
@@ -514,7 +510,9 @@
     srow[64:80, :] = jnp.ones((16, 512), BF16)
     which = sub[0:32]
 
-    def decode(j, carry):
+    def decode(u, carry):
+        dz, dx = points_offset(NY - 1 - u)
+        j = peer(dz, dx)
         nums, dens = [], []
         for i in range(CAP):
             o = dot(srow[...], kst[j * CAP + i])
@@ -523,16 +521,18 @@
             nums.append(total(jnp.where(owned, o[0:32] + o[32:64], 0.0)))
             dens.append(o[64:65])
         psend[pl.ds(pl.multiple_of(j * CAP, CAP), CAP), :] = jnp.concatenate(nums, axis=0) / jnp.concatenate(dens, axis=0)
+
+        @pl.when(u < NY - 1)
+        def _():
+            pltpu.make_async_remote_copy(
+                src_ref=psend.at[pl.ds(pl.multiple_of(j * CAP, CAP), CAP), :], dst_ref=precv.at[mine, :],
+                send_sem=rsem.at[0], recv_sem=rsem.at[1], device_id=(gx, j), device_id_type=MESH,
+            ).start()
+
         return carry
 
     lax.fori_loop(0, NY, decode, 0)
     precv[mine, :] = psend[mine, :]
-    for dz, dx in FAR[:-1]:
-        j = peer(dz, dx)
-        pltpu.make_async_remote_copy(
-            src_ref=psend.at[pl.ds(pl.multiple_of(j * CAP, CAP), CAP), :], dst_ref=precv.at[mine, :],
-            send_sem=rsem.at[0], recv_sem=rsem.at[1], device_id=(gx, j), device_id_type=MESH,
-        ).start()
     part = precv.at[pl.ds(0, (NY - 1) * CAP), :]
     pltpu.make_async_copy(part, part, rsem.at[1]).wait()
     pltpu.make_async_copy(part, part, rsem.at[0]).wait()

time: 105 us -> 102 us (0.971)
  Pallas kernels: 103 us -> 99.2 us
    pallas_call x1, Pallas kernels: 103 us -> 99.2 us  [per_device(): pl.pallas_call(mega, out_shape=jax.ShapeDtypeStruct((SLOTS, 128), F32), i...]
where the time goes in v3:
time: 102 us; the launch traced here: 101 us
  Pallas kernels  99.2 us (97%)
  local copies, waits for them, and re-layouts  1.47 us (1%)
    pallas_call x1, Pallas kernels, per_device(): pl.pallas_call(mega, out_shape=jax.ShapeDtypeStruct((SLOTS, 128), F32), i...  99.2 us

profile of v3, /device:TPU:0, one launch (start us, length us, event | category | flops | bytes accessed | tf_op | source)
XLA Modules:
  0.0 101.3 jit_solution(14830174199553100450)
XLA Ops:
  0.7 99.2 %operator.1 = f32[128,128]{1,0:T(8,128)} custom-call(s32[1,128]{1,0:T(1,128)} %bitcast.9, s32[1]{0:T(128)S(6)} %copy.20.count, f32[32,16384]{1,0:T(8,128)} %feat.1, f32[3,16384]{1,0:T(4,128)} %pos.1, f32[1,16384]{1,0:T(1,128)} %bitcast.6, f32[128,128]{1,0:T(8,128)} %bitcast.7, f32[32]{0:T(128)} %gain.1, f32[2,32,32]{2,1,0:T(8,128)} %mix.1, f32[2,32]{1,0:T(2,128)} %bias.1, ...), custom_call_target="tpu_custom_call" | custom-call | tf_op jit(solution)/shard_map/operator/pallas_call | solution.py:551
  99.8 1.5 %copy.21 = f32[16384]{0:T(1024)} copy(f32[16384]{0:T(1024)} %bitcast.5) | data formatting | bytes 131072
